TPU v7x, 1024 devices: a whole 8x8x8 slice. The times are simulated.
1024 devices in a mesh: seq: 16 (over x, core), dp: 64 (over y, z).
Axes of the slice: x: 8, y: 8, z: 8, core: 2. Of those that a mesh axis runs over, the one named last changes fastest.
Arguments:
- queries: bfloat16 [64, 2048, 4096], P('dp', 'seq'), may hold values from -6 to 6
- keys: bfloat16 [64, 2048, 512], P('dp', 'seq'), may hold values from -6 to 6
- values: bfloat16 [64, 2048, 512], P('dp', 'seq'), may hold values from -6 to 6
- grad_out: bfloat16 [64, 2048, 4096], P('dp', 'seq'), may hold values from -6 to 6
- features: bfloat16 [64, 2048, 4096], P('dp', 'seq'), may hold values from -100 to 100
- doc_lengths: int32 [64, 32], P('dp'), may hold values from 1 to 128, 2048 in all within a row
Outputs:
- key_grad: bfloat16 [64, 2048, 512], P('dp', 'seq')
- clipped_grad: float32 [4096, 512], P(('seq', 'dp'))
Inputs may be any that keep to these rules, and one draw needn't show every extreme that they name: `doc_lengths`: each row sums to 2048; the longest document of every data group has exactly 128 tokens.
All inputs are finite; a program needn't handle non-finite values.
Results may differ from a plain program's by a relative error of at most 0.0058.
Values may be sent and summed in bfloat16 or wider, within the bound.
A program may use at most 32 MiB of HBM per device.

v0:
```python
import math

import jax
import jax.numpy as jnp
from jax import lax
from jax.sharding import PartitionSpec as P

HD = 128
HQ = 32
KVH = 4
DW = 4096
DOC_MAX = 128
QBLK = 512


NEG_FILL = -1e30


def doc_index(lengths, positions):
    doc_ends = jnp.cumsum(lengths, dtype=jnp.int32)
    located = jnp.sum((doc_ends[None, :] <= positions[:, None]).astype(jnp.int32), axis=1)
    return jnp.where(positions < 0, -1, located)


def shards(queries, keys, values, grad_out, features, doc_lengths):
    seq_count = lax.axis_size("seq")
    tok_rows = queries.shape[1]
    slab_len = tok_rows * seq_count
    local_heads = HQ // seq_count
    sharers = seq_count // KVH
    block_rows = DW // seq_count
    score_scale = 1.0 / math.sqrt(HD)
    block_width = QBLK + DOC_MAX
    query_send = queries[0].reshape(tok_rows, seq_count, local_heads * HD)
    grad_send = grad_out[0].reshape(tok_rows, seq_count, local_heads * HD)
    query_heads, grad_heads = (
        lax.all_to_all(query_send, "seq", split_axis=1, concat_axis=0, tiled=True),
        lax.all_to_all(grad_send, "seq", split_axis=1, concat_axis=0, tiled=True),
    )
    query_heads = query_heads.reshape(slab_len, local_heads, HD)
    grad_heads = grad_heads.reshape(slab_len, local_heads, HD)
    key_three = keys[0].reshape(tok_rows, KVH, HD)
    value_three = values[0].reshape(tok_rows, KVH, HD)
    pair_send = jnp.repeat(jnp.concatenate([key_three, value_three], axis=2), sharers, axis=1)
    feature_send = features[0].reshape(tok_rows, seq_count, block_rows)
    pair_heads, feature_cols = (
        lax.all_to_all(pair_send, "seq", split_axis=1, concat_axis=0, tiled=True),
        lax.all_to_all(feature_send, "seq", split_axis=1, concat_axis=0, tiled=True),
    )
    feature_block = feature_cols.reshape(slab_len, block_rows)
    pair_heads = pair_heads.reshape(slab_len, 2 * HD)
    key_pad = jnp.concatenate([jnp.zeros((DOC_MAX, 2 * HD), jnp.bfloat16), pair_heads], axis=0)
    lengths = doc_lengths[0]

    def one_block(block_index, key_total):
        row_start = (block_index * QBLK).astype(jnp.int32)
        query_rows = lax.dynamic_slice_in_dim(query_heads, row_start, QBLK, 0)
        grad_rows = lax.dynamic_slice_in_dim(grad_heads, row_start, QBLK, 0)
        window = lax.dynamic_slice_in_dim(key_pad, row_start, block_width, 0)
        key_window = window[:, :HD]
        value_window = window[:, HD:]
        query_pos = row_start + jnp.arange(QBLK, dtype=jnp.int32)
        key_pos = row_start - DOC_MAX + jnp.arange(block_width, dtype=jnp.int32)
        query_doc = doc_index(lengths, query_pos)
        key_doc = doc_index(lengths, key_pos)
        visible = (query_doc[:, None] == key_doc[None, :]) & (
            key_pos[None, :] <= query_pos[:, None]
        )
        scores = (
            jnp.einsum("qhd,kd->hqk", query_rows, key_window, preferred_element_type=jnp.float32)
            * score_scale
        )
        scores = jnp.where(visible[None], scores, NEG_FILL)
        row_peak = jnp.max(scores, axis=2, keepdims=True)
        exponent = jnp.exp(scores - row_peak)
        attention = exponent / jnp.sum(exponent, axis=2, keepdims=True)
        grad_weights = jnp.einsum(
            "qhd,kd->hqk", grad_rows, value_window, preferred_element_type=jnp.float32
        )
        row_delta = jnp.sum(attention * grad_weights, axis=2, keepdims=True)
        grad_scores = (attention * (grad_weights - row_delta) * score_scale).astype(jnp.bfloat16)
        contribution = jnp.einsum(
            "hqk,qhd->kd", grad_scores, query_rows, preferred_element_type=jnp.float32
        )
        current = lax.dynamic_slice_in_dim(key_total, row_start, block_width, 0)
        return lax.dynamic_update_slice_in_dim(key_total, current + contribution, row_start, 0)

    key_total = lax.fori_loop(
        0, slab_len // QBLK, one_block, jnp.zeros((DOC_MAX + slab_len, HD), jnp.float32)
    )
    key_part = key_total[DOC_MAX:].astype(jnp.bfloat16)
    key_back = lax.all_to_all(key_part, "seq", split_axis=0, concat_axis=1, tiled=True)
    key_sum = jnp.sum(key_back.reshape(tok_rows, KVH, sharers, HD).astype(jnp.float32), axis=2)
    key_grad = key_sum.reshape(tok_rows, KVH * HD).astype(jnp.bfloat16)
    weight_part = lax.dot_general(
        feature_block,
        lax.all_gather(key_grad, "seq", axis=0, tiled=True),
        (((0,), (0,)), ((), ())),
        preferred_element_type=jnp.float32,
    )
    entry_count = DW * KVH * HD
    own_rows = lax.psum_scatter(weight_part, "dp", scatter_dimension=0, tiled=True)
    squares = lax.psum(jnp.sum(own_rows * own_rows), ("seq", "dp"))
    root_mean = jnp.sqrt(squares / entry_count + 1e-06)
    clipped_grad = own_rows * jnp.minimum(1.0, 1.0 / root_mean)
    return (key_grad[None], clipped_grad)


def solution(mesh):
    in_specs = (
        P("dp", "seq", None),
        P("dp", "seq", None),
        P("dp", "seq", None),
        P("dp", "seq", None),
        P("dp", "seq", None),
        P("dp", None),
    )
    out_specs = (P("dp", "seq", None), P(("seq", "dp"), None))
    return jax.shard_map(shards, mesh=mesh, in_specs=in_specs, out_specs=out_specs, check_vma=False)
```

profile of v0, /device:TPU:1, one launch (start us, length us, event | category | flops | bytes accessed | tf_op | source)
XLA Modules:
  0.0 532.7 jit_solution(9107467584689674496)
XLA Ops:
  7.2 2.4 copy.48
  9.5 17.6 %all-to-all-start.1 = ((bf16[128,16,256]{0,2,1:T(8,128)(2,1)}), bf16[128,16,256]{0,2,1:T(8,128)(2,1)S(1)}, u32[]{:S(2)}, u32[]{:S(2)}) async-start(bf16[128,16,256]{0,2,1:T(8,128)(2,1)} %bitcast.10), calls=%async_computation.1 | async-start | bytes 2097152 | tf_op jit(solution)/shard_map/all_to_all | solution.py:37
  27.1 1.3 copy.50
  28.5 26.7 %all-to-all-done.1 = bf16[128,16,256]{0,2,1:T(8,128)(2,1)S(1)} async-done(((bf16[128,16,256]{0,2,1:T(8,128)(2,1)}), bf16[128,16,256]{0,2,1:T(8,128)(2,1)S(1)}, u32[]{:S(2)}, u32[]{:S(2)}) %all-to-all-start.1) | async-done | bytes 1048608 | tf_op jit(solution)/shard_map/all_to_all | solution.py:37
  55.1 3.6 all-to-all-start.2
  59.0 27.6 %all-to-all-done.2 = bf16[128,16,256]{0,2,1:T(8,128)(2,1)S(1)} async-done(((bf16[128,16,256]{0,2,1:T(8,128)(2,1)}), bf16[128,16,256]{0,2,1:T(8,128)(2,1)S(1)}, u32[]{:S(2)}, u32[]{:S(2)}) %all-to-all-start.2) | async-done | bytes 1048608 | tf_op jit(solution)/shard_map/all_to_all | solution.py:38
  87.7 3.5 all-to-all-start
  91.5 1.7 copy.49
  93.2 2.3 reshape.155
  96.2 1.3 reshape.156
  97.5 21.6 %all-to-all-done = bf16[128,16,256]{2,0,1:T(8,128)(2,1)S(1)} async-done(((bf16[128,16,256]{2,0,1:T(8,128)(2,1)}), bf16[128,16,256]{2,0,1:T(8,128)(2,1)S(1)}, u32[]{:S(2)}, u32[]{:S(2)}) %all-to-all-start) | async-done | bytes 1048608 | tf_op jit(solution)/shard_map/all_to_all | solution.py:47
  121.3 40.8 %while.15 = (s32[]{:T(128)}, f32[2176,128]{1,0:T(8,128)}, s32[1,32]{1,0:T(1,128)S(1)}, bf16[2176,256]{1,0:T(8,128)(2,1)}, bf16[2048,2,128]{0,2,1:T(8,128)(2,1)},...) while((s32[]{:T(128)}, f32[2176,128]{1,0:T(8,128)}, ...), condition=%wide.region_7.8_spmd, body=%wide.region_1.7_spmd.sunk | while | flops 510398720 | bytes 18186248 | solution.py:88
  121.8 4.0 fusion.58
  125.8 1.5 fusion.59
  127.3 4.1 fusion.60
  132.0 4.0 fusion.58
  136.0 1.5 fusion.59
  137.5 4.1 fusion.60
  142.2 4.0 fusion.58
  146.2 1.5 fusion.59
  147.7 4.1 fusion.60
  152.4 4.0 fusion.58
  156.4 1.5 fusion.59
  157.9 4.1 fusion.60
  162.1 1.4 slice.27
  163.4 20.4 %all_to_all.73 = bf16[16,128,128]{2,1,0:T(8,128)(2,1)S(1)} all-to-all(bf16[16,128,128]{2,1,0:T(8,128)(2,1)S(1)} %bitcast.105), channel_id=1, replica_groups=mesh['seq'=16,'dp'=64] {'seq'}, dimensions={0} | all-to-all | bytes 1048576 | tf_op jit(solution)/shard_map/all_to_all | solution.py:92
  185.5 34.5 %all_to_all.74 = bf16[128,16,256]{0,2,1:T(8,128)(2,1)S(1)} all-to-all(bf16[128,16,256]{0,2,1:T(8,128)(2,1)S(1)} %bitcast.104), channel_id=1, replica_groups=mesh['seq'=16,'dp'=64] {'seq'}, dimensions={1} | all-to-all | bytes 2097152 | tf_op jit(solution)/shard_map/all_to_all | solution.py:48
  220.5 16.1 %all-gather.2.cloned.1.call-done = bf16[2048,512]{0,1:T(8,128)(2,1)} async-done(((bf16[128,512]{0,1:T(8,128)(2,1)}), bf16[2048,512]{0,1:T(8,128)(2,1)}) %all-gather.2.cloned.1.call-update) | async-done | bytes 2097168 | tf_op jit(solution)/shard_map/all_gather | solution.py:97
  236.6 3.1 convolution_bitcast_fusion
  241.6 163.8 %all-reduce.4.cloned.1.call-done = f32[256,512]{0,1:T(8,128)} async-done(((f32[256,512]{0,1:T(8,128)}), f32[256,512]{0,1:T(8,128)}) %all-reduce.4.cloned.1.call-update) | async-done | bytes 524304
  405.4 1.7 multiply_reduce_fusion
  407.9 115.4 %psum.7 = f32[]{:T(128)} all-reduce(f32[]{:T(128)} %multiply_reduce_fusion), channel_id=1, replica_groups=mesh['seq'=16,'dp'=64] {'seq','dp'}, use_global_device_ids=true, to_apply=%region_11.12 | all-reduce | flops 1 | bytes 8 | tf_op jit(solution)/shard_map/psum | solution.py:103
  (61 shorter events, 12.5 us)
Async XLA Ops:
  7.2 19.9 %copy-start.1 = (bf16[1,128,4096]{2,1,0:T(8,128)(2,1)S(1)}, bf16[1,128,4096]{2,1,0:T(8,128)(2,1)}, u32[]{:S(2)}) copy-start(bf16[1,128,4096]{2,1,0:T(8,128)(2,1)} %param.11) | copy-start | bytes 3145732
  9.5 45.6 %all-to-all-start.1 = ((bf16[128,16,256]{0,2,1:T(8,128)(2,1)}), bf16[128,16,256]{0,2,1:T(8,128)(2,1)S(1)}, u32[]{:S(2)}, u32[]{:S(2)}) async-start(bf16[128,16,256]{0,2,1:T(8,128)(2,1)} %bitcast.10), calls=%async_computation.1 | async-start | bytes 2097152 | tf_op jit(solution)/shard_map/all_to_all | solution.py:37
  27.1 31.6 %copy-start.3 = (bf16[1,128,512]{2,1,0:T(8,128)(2,1)S(1)}, bf16[1,128,512]{2,1,0:T(8,128)(2,1)}, u32[]{:S(2)}) copy-start(bf16[1,128,512]{2,1,0:T(8,128)(2,1)} %param.9) | copy-start | bytes 393220
  27.1 31.6 %copy-start.4 = (bf16[1,128,512]{2,1,0:T(8,128)(2,1)S(1)}, bf16[1,128,512]{2,1,0:T(8,128)(2,1)}, u32[]{:S(2)}) copy-start(bf16[1,128,512]{2,1,0:T(8,128)(2,1)} %param.10) | copy-start | bytes 393220
  55.1 31.4 %all-to-all-start.2 = ((bf16[128,16,256]{0,2,1:T(8,128)(2,1)}), bf16[128,16,256]{0,2,1:T(8,128)(2,1)S(1)}, u32[]{:S(2)}, u32[]{:S(2)}) async-start(bf16[128,16,256]{0,2,1:T(8,128)(2,1)} %bitcast.13), calls=%async_computation.2 | async-start | bytes 2097152 | tf_op jit(solution)/shard_map/all_to_all | solution.py:38
  58.7 32.6 %copy-start.5 = (s32[1,32]{1,0:T(1,128)S(1)}, s32[1,32]{1,0:T(1,128)}, u32[]{:S(2)}) copy-start(s32[1,32]{1,0:T(1,128)} %param.13) | copy-start | bytes 388
  87.7 31.4 %all-to-all-start = ((bf16[128,16,256]{2,0,1:T(8,128)(2,1)}), bf16[128,16,256]{2,0,1:T(8,128)(2,1)S(1)}, u32[]{:S(2)}, u32[]{:S(2)}) async-start(bf16[128,16,256]{2,0,1:T(8,128)(2,1)} %bitcast.6), calls=%async_computation | async-start | bytes 2097152 | tf_op jit(solution)/shard_map/all_to_all | solution.py:47
  91.2 145.4 %all-gather.2.cloned.1.call-start = ((), (), s32[]{:S(2)}) async-start(), calls=%async_computation.5 | async-start | bytes 2228224 | tf_op jit(solution)/shard_map/all_gather | solution.py:97
  162.1 22.7 %copy-start.2 = (bf16[1,128,4096]{2,1,0:T(8,128)(2,1)S(1)}, bf16[1,128,4096]{2,1,0:T(8,128)(2,1)}, u32[]{:S(2)}) copy-start(bf16[1,128,4096]{2,1,0:T(8,128)(2,1)} %param.12) | copy-start | bytes 3145732
  184.7 220.7 %all-reduce.4.cloned.1.call-start = ((), (), s32[]{:S(2)}) async-start(), calls=%async_computation.6 | async-start | bytes 1048576
  220.5 186.6 %copy-start = (bf16[128,4,128]{0,2,1:T(8,128)(2,1)S(1)}, bf16[128,4,128]{0,2,1:T(8,128)(2,1)}, u32[]{:S(2)}) copy-start(bf16[128,4,128]{0,2,1:T(8,128)(2,1)} %copy.54) | copy-start | bytes 393220
Sparse Core Ops, SparseCore 0:
  184.9 51.6 all-gather.1
  239.8 165.5 all-reduce.3
where the time goes:
time: 534 us; the launch traced here: 533 us
  waiting for transfers between devices  256 us (48%)
  blocking collectives  170 us (32%)
  matrix products  41.6 us (8%)
  starting transfers between devices  24.7 us (5%)
  local copies, waits for them, and re-layouts  19.2 us (4%)
  between operations  15.5 us (3%)
    unnamed x3, waiting for transfers between devices  164 us
    psum x1, blocking collectives, shards(): squares = lax.psum(jnp.sum(own_rows * own_rows), ('seq', 'dp'))  115 us
    all_to_all x1, blocking collectives, shards(): lax.all_to_all(feature_send, 'seq', split_axis=1, concat_axis=0, tiled=True)  34.5 us
    all_to_all x1, waiting for transfers between devices, shards(): lax.all_to_all(grad_send, 'seq', split_axis=1, concat_axis=0, tiled=True)  27.6 us
    all_to_all x1, waiting for transfers between devices, shards(): lax.all_to_all(query_send, 'seq', split_axis=1, concat_axis=0, tiled=True)  26.7 us
    all_to_all x1, waiting for transfers between devices, shards(): lax.all_to_all(pair_send, 'seq', split_axis=1, concat_axis=0, tiled=True)  21.6 us
    all_to_all x1, blocking collectives, shards(): lax.all_to_all(key_part, 'seq', split_axis=0, concat_axis=1, tiled=True)  20.4 us
    all_to_all x1, starting transfers between devices, shards(): lax.all_to_all(query_send, 'seq', split_axis=1, concat_axis=0, tiled=True)  17.6 us
  transfers between devices with their start and end apart: 5, of which 5 were waited for; matrix products, arithmetic and copies ran while one was open for 2% of the time, Pallas kernels for 0%

commit v1 on v0

v1 whole, which is shorter than its diff:
```python
import functools
import math

import jax
import jax.numpy as jnp
from jax import lax
from jax.experimental import pallas as pl
from jax.experimental.pallas import tpu as pltpu
from jax.sharding import PartitionSpec as P

HD = 128
KVH = 4
NEG_FILL = -1e30
MESH = pl.DeviceIdType.MESH
Z_CHIPS = 8
SUBS = 2


def kernel(
    dims, q_ref, k_ref, v_ref, do_ref, f_ref, len_ref, kg_ref, w_ref,
    k_prev, v_prev, grad_cols, key_own, back_send, back_recv,
    feat_cols, feat_send, pair_grad, weight, ring_send, ring_recv,
    mid_send, mid_recv, last_send, last_recv, sq_send, sq_recv,
    halo_sems, feat_sems, back_sems, pair_sems, ring_sems, mid_sems, last_sems, sq_sems,
):
    nx, ny, nz, rows, entry_count = dims
    tok = q_ref.shape[0]
    width = k_ref.shape[1]
    heads = q_ref.shape[1] // width
    half = width // 2
    sub = half // SUBS
    score_scale = 1.0 / math.sqrt(HD)

    seq, dp = lax.axis_index("seq"), lax.axis_index("dp")
    x, core = seq // 2, seq % 2
    y, z = dp // nz, dp % nz
    count = nx * 2
    right = (lax.rem(seq + 1, count), dp)
    left = (lax.rem(seq + count - 1, count), dp)
    partner = (x * 2 + 1 - core, dp)

    def at_x(step):
        return (lax.rem(x + step, nx) * 2 + core, dp)

    def at_y(step):
        return (seq, lax.rem(y + step, ny) * nz + z)

    def at_z(step):
        return (seq, y * nz + lax.rem(z + step, nz))

    barrier = pltpu.get_barrier_semaphore()
    pl.semaphore_signal(barrier, inc=1, device_id=left, device_id_type=MESH)
    pl.semaphore_signal(barrier, inc=1, device_id=right, device_id_type=MESH)
    for where_to, size in ((at_x, nx), (at_y, ny), (at_z, nz)):
        def greet(step, carry, where_to=where_to):
            pl.semaphore_signal(barrier, inc=1, device_id=where_to(step), device_id_type=MESH)
            return carry
        lax.fori_loop(1, size, greet, 0)

    def turn(block, carry):
        here = pl.multiple_of((block * 2 + core) * feat_cols.shape[1], 128)
        there = pl.multiple_of((block * 2 + 1 - core) * feat_cols.shape[1], 128)
        feat_cols[block, :, 0:tok] = f_ref[:, pl.ds(here, feat_cols.shape[1])].T
        feat_send[block] = f_ref[:, pl.ds(there, feat_cols.shape[1])].T
        return carry

    lax.fori_loop(0, nx, turn, 0)
    pl.semaphore_wait(barrier, 2 + (nx - 1) + (ny - 1) + (nz - 1))

    def remote(src, dst, sems, place, target):
        return pltpu.make_async_remote_copy(
            src_ref=src, dst_ref=dst, send_sem=sems.at[(0,) + place], recv_sem=sems.at[(1,) + place],
            device_id=target, device_id_type=MESH,
        )

    key_copy = remote(k_ref, k_prev, halo_sems, (0,), right)
    value_copy = remote(v_ref, v_prev, halo_sems, (1,), right)
    feat_copy = remote(feat_send, feat_cols.at[:, :, pl.ds(tok, tok)], feat_sems, (0,), partner)
    key_copy.start()
    value_copy.start()
    feat_copy.start()

    query_pos = seq * tok + lax.broadcasted_iota(jnp.int32, (1, tok), 1)
    key_pos = (seq - 1) * tok + lax.broadcasted_iota(jnp.int32, (2 * tok, tok), 0)

    def doc_start(doc, carry):
        total, start = carry
        total = total + len_ref[0, doc]
        return total, jnp.where(query_pos >= total, total, start)

    first_key = lax.fori_loop(0, len_ref.shape[1], doc_start, (jnp.int32(0), jnp.zeros((1, tok), jnp.int32)))[1]
    visible = (key_pos >= first_key) & (key_pos <= query_pos)

    key_copy.wait_recv()
    value_copy.wait_recv()

    def back_copy(group):
        return remote(back_send.at[group], back_recv.at[group], back_sems, (group,), left)

    def one_group(group, carry):
        cols = pl.ds(pl.multiple_of(group * HD, HD), HD)
        keys = jnp.concatenate([k_prev[:, cols], k_ref[:, cols]], axis=0)
        values = jnp.concatenate([v_prev[:, cols], v_ref[:, cols]], axis=0)
        queries = []
        for head in range(heads):
            at = pl.ds(pl.multiple_of((group * heads + head) * HD, HD), HD)
            query = q_ref[:, at]
            queries.append(query)
            scores = lax.dot_general(
                keys, query, (((1,), (1,)), ((), ())), preferred_element_type=jnp.float32
            ) * score_scale
            grad_weights = lax.dot_general(
                values, do_ref[:, at], (((1,), (1,)), ((), ())), preferred_element_type=jnp.float32
            )
            scores = jnp.where(visible, scores, NEG_FILL)
            exponent = jnp.exp(scores - jnp.max(scores, axis=0, keepdims=True))
            attention = exponent * (1.0 / jnp.sum(exponent, axis=0, keepdims=True))
            row_delta = jnp.sum(attention * grad_weights, axis=0, keepdims=True)
            grad_cols[:, head * HD:(head + 1) * HD] = (
                attention * (grad_weights - row_delta) * score_scale
            ).astype(jnp.bfloat16)
        key_part = jnp.dot(
            grad_cols[...], jnp.concatenate(queries, axis=0), preferred_element_type=jnp.float32
        )
        back_send[group] = key_part[:tok].astype(jnp.bfloat16)
        key_own[:, cols] = key_part[tok:]
        back_copy(group).start()
        return carry

    lax.fori_loop(0, KVH, one_group, 0)

    def add_back(group, carry):
        cols = pl.ds(pl.multiple_of(group * HD, HD), HD)
        back_copy(group).wait()
        done = (key_own[:, cols] + back_recv[group].astype(jnp.float32)).astype(jnp.bfloat16)
        kg_ref[:, cols] = done
        pair_grad[0:tok, cols] = done
        return carry

    lax.fori_loop(0, KVH, add_back, 0)
    pair_copy = remote(
        pair_grad.at[pl.ds(0, tok)], pair_grad.at[pl.ds(tok, tok)], pair_sems, (0,), partner
    )
    pair_copy.start()
    key_copy.wait_send()
    value_copy.wait_send()
    feat_copy.wait()
    pair_copy.wait()

    def multiply(block, carry):
        weight[block] = jnp.dot(
            feat_cols[block], pair_grad[...], preferred_element_type=jnp.float32
        ).reshape(weight.shape[1:])
        return carry

    lax.fori_loop(0, nx, multiply, 0)

    sides = (
        (0, nx, at_x, lambda step, cols: weight[lax.rem(x + step + nx, nx), :, :, cols]),
        (1, ny, at_y, lambda step, cols: weight[:, lax.rem(y + step + ny, ny), :, cols]),
    )

    others = (pl.ds(0, ny), pl.ds(0, nx))

    def ring_copy(side, way, piece, step, where_to, size):
        target = where_to(size - 1) if way == 0 else where_to(1)
        place = (side, way, piece, step, others[side])
        return remote(ring_send.at[place], ring_recv.at[place], ring_sems, place[:4], target)

    def reach(way, size):
        return size // 2 if way == 0 else (size - 1) // 2

    def columns(side, piece):
        return pl.ds(side * half + piece * sub, sub)

    most = max(nx, ny) // 2
    for step in range(most):
        for piece in range(SUBS):
            for way in range(2):
                for side, size, where_to, own in sides:
                    far = reach(way, size)
                    if step >= far:
                        continue
                    away = (step - far) if way == 0 else (far - step)
                    term = own(away, columns(side, piece))
                    if step > 0:
                        ring_copy(side, way, piece, step - 1, where_to, size).wait_recv()
                        term = term + ring_recv[side, way, piece, step - 1, others[side]].astype(jnp.float32)
                    ring_send[side, way, piece, step, others[side]] = term.astype(jnp.bfloat16)
                    ring_copy(side, way, piece, step, where_to, size).start()

    def mid_copy(side, step):
        where_to = at_y if side == 0 else at_x
        size = ny if side == 0 else nx
        index = lax.rem((y if side == 0 else x) + step, size)
        return remote(
            mid_send.at[side, index], mid_recv.at[side, step], mid_sems, (side, step), where_to(step)
        )

    sums = []
    for side, size, where_to, own in sides:
        pieces = []
        for piece in range(SUBS):
            term = own(0, columns(side, piece))
            for way in range(2):
                far = reach(way, size)
                if far:
                    ring_copy(side, way, piece, far - 1, where_to, size).wait_recv()
                    term = term + ring_recv[side, way, piece, far - 1, others[side]].astype(jnp.float32)
            pieces.append(term)
        whole = jnp.concatenate(pieces, axis=2)
        mid_send[side, others[side]] = whole.astype(jnp.bfloat16)
        other = ny if side == 0 else nx
        def send_mid(step, carry, side=side):
            mid_copy(side, step).start()
            return carry
        lax.fori_loop(1, other, send_mid, 0)
    for side, size, where_to, own in sides:
        other = ny if side == 0 else nx
        def add_mid(step, carry, side=side):
            mid_copy(side, step).wait_recv()
            return carry + mid_recv[side, step].astype(jnp.float32)
        mine = mid_send[side, y if side == 0 else x].astype(jnp.float32)
        sums.append(lax.fori_loop(1, other, add_mid, mine))
    block = jnp.concatenate(sums, axis=1)

    for index in range(nz):
        last_send[index] = block[index * rows:(index + 1) * rows]

    def last_copy(step):
        return remote(
            last_send.at[lax.rem(z + step, nz)], last_recv.at[step], last_sems, (step,), at_z(step)
        )

    def send_last(step, carry):
        last_copy(step).start()
        return carry

    def add_last(step, carry):
        last_copy(step).wait_recv()
        return carry + last_recv[step]

    lax.fori_loop(1, nz, send_last, 0)
    own_rows = lax.fori_loop(1, nz, add_last, last_send[z])

    squares = jnp.sum(own_rows * own_rows, axis=0, keepdims=True)
    squares = jnp.broadcast_to(
        jnp.sum(squares.reshape(1, width // HD, HD), axis=1), (8, HD)
    )
    axes = ((at_z, nz), (at_y, ny), (at_x, nx), (lambda step: partner, 2))
    for stage, (where_to, size) in enumerate(axes):
        sq_send[stage] = squares
        def sq_copy(step, stage=stage, where_to=where_to):
            return remote(sq_send.at[stage], sq_recv.at[stage, step], sq_sems, (stage, step), where_to(step))
        def send_sq(step, carry):
            sq_copy(step).start()
            return carry
        def add_sq(step, carry, stage=stage):
            sq_copy(step).wait_recv()
            return carry + sq_recv[stage, step]
        lax.fori_loop(1, size, send_sq, 0)
        squares = lax.fori_loop(1, size, add_sq, squares)
    total = jnp.sum(squares[0:1], axis=1, keepdims=True)
    root_mean = jnp.sqrt(total / entry_count + 1e-06)
    w_ref[...] = own_rows * jnp.minimum(1.0, 1.0 / root_mean)

    for step in range(most):
        for piece in range(SUBS):
            for way in range(2):
                for side, size, where_to, own in sides:
                    if step < reach(way, size):
                        ring_copy(side, way, piece, step, where_to, size).wait_send()
    for side in range(2):
        def end_mid(step, carry, side=side):
            mid_copy(side, step).wait_send()
            return carry
        lax.fori_loop(1, ny if side == 0 else nx, end_mid, 0)

    def end_last(step, carry):
        last_copy(step).wait_send()
        return carry

    lax.fori_loop(1, nz, end_last, 0)
    for stage, (where_to, size) in enumerate(axes):
        def end_sq(step, carry, stage=stage, where_to=where_to):
            remote(
                sq_send.at[stage], sq_recv.at[stage, step], sq_sems, (stage, step), where_to(step)
            ).wait_send()
            return carry
        lax.fori_loop(1, size, end_sq, 0)


def shards(sizes, queries, keys, values, grad_out, features, doc_lengths):
    seq_count, dp_count = sizes
    nz = min(Z_CHIPS, dp_count)
    nx, ny = seq_count // 2, dp_count // nz
    tok, wide = features.shape[1:]
    width = keys.shape[2]
    rows = wide // (seq_count * dp_count)
    low = nz * rows
    most = max(nx, ny)
    sub = width // 2 // SUBS
    dma = pltpu.SemaphoreType.DMA
    vmem = pl.BlockSpec(memory_space=pltpu.VMEM)
    bf16, f32 = jnp.bfloat16, jnp.float32
    key_grad, clipped = pl.pallas_call(
        functools.partial(kernel, (nx, ny, nz, rows, wide * width)),
        out_shape=(
            jax.ShapeDtypeStruct((tok, width), bf16),
            jax.ShapeDtypeStruct((rows, width), f32),
        ),
        in_specs=[vmem] * 5 + [pl.BlockSpec(memory_space=pltpu.SMEM)],
        out_specs=(vmem, vmem),
        scratch_shapes=[
            pltpu.VMEM((tok, width), bf16),
            pltpu.VMEM((tok, width), bf16),
            pltpu.VMEM((2 * tok, queries.shape[2] // KVH), bf16),
            pltpu.VMEM((tok, width), f32),
            pltpu.VMEM((KVH, tok, HD), bf16),
            pltpu.VMEM((KVH, tok, HD), bf16),
            pltpu.VMEM((nx, ny * low, 2 * tok), bf16),
            pltpu.VMEM((nx, ny * low, tok), bf16),
            pltpu.VMEM((2 * tok, width), bf16),
            pltpu.VMEM((nx, ny, low, width), f32),
            pltpu.VMEM((2, 2, SUBS, most // 2, most, low, sub), bf16),
            pltpu.VMEM((2, 2, SUBS, most // 2, most, low, sub), bf16),
            pltpu.VMEM((2, most, low, width // 2), bf16),
            pltpu.VMEM((2, most, low, width // 2), bf16),
            pltpu.VMEM((nz, rows, width), f32),
            pltpu.VMEM((nz, rows, width), f32),
            pltpu.VMEM((4, 8, HD), f32),
            pltpu.VMEM((4, max(most, nz), 8, HD), f32),
            dma((2, 2)),
            dma((2, 1)),
            dma((2, KVH)),
            dma((2, 1)),
            dma((2, 2, 2, SUBS, most // 2)),
            dma((2, 2, most)),
            dma((2, nz)),
            dma((2, 4, max(most, nz))),
        ],
        compiler_params=pltpu.CompilerParams(
            collective_id=0, has_side_effects=True, vmem_limit_bytes=48 << 20
        ),
    )(queries[0], keys[0], values[0], grad_out[0], features[0], doc_lengths)
    return key_grad[None], clipped


def solution(mesh):
    in_specs = (
        P("dp", "seq", None),
        P("dp", "seq", None),
        P("dp", "seq", None),
        P("dp", "seq", None),
        P("dp", "seq", None),
        P("dp", None),
    )
    out_specs = (P("dp", "seq", None), P(("seq", "dp"), None))
    return jax.shard_map(
        functools.partial(shards, (mesh.shape["seq"], mesh.shape["dp"])),
        mesh=mesh, in_specs=in_specs, out_specs=out_specs, check_vma=False,
    )
```

time: 534 us -> 93.3 us (0.17)
  waiting for transfers between devices: 256 us -> 0 us
  blocking collectives: 170 us -> 0 us
  Pallas kernels: 0 us -> 85 us
  matrix products: 41.6 us -> 0 us
  starting transfers between devices: 24.7 us -> 0 us
  between operations: 15.5 us -> 0.65 us
  local copies, waits for them, and re-layouts: 19.2 us -> 7.38 us
    unnamed x3 -> x0, waiting for transfers between devices: 164 us -> none
    psum x1 -> x0, blocking collectives: 115 us -> none  [shards(): squares = lax.psum(jnp.sum(own_rows * own_rows), ('seq', 'dp'))]
    pallas_call x0 -> x1, Pallas kernels: none -> 85 us  [shards(): pl.pallas_call(functools.partial(kernel, (nx, ny, nz, rows, wide * width)...]
    all_to_all x3 -> x0, waiting for transfers between devices: 75.9 us -> none  [the longest x1 27.6 us: shards(): lax.all_to_all(grad_send, 'seq', split_axis=1, concat_axis=0, tiled=True)]
    all_to_all x2 -> x0, blocking collectives: 54.9 us -> none  [the longest x1 34.5 us: shards(): lax.all_to_all(feature_send, 'seq', split_axis=1, concat_axis=0, tiled=True)]
    dot_general x9 -> x0, matrix products: 25.6 us -> none  [the longest x4 16.5 us: one_block(): jnp.einsum('hqk,qhd->kd', grad_scores, query_rows, preferred_element_type...]
    all_to_all x3 -> x0, starting transfers between devices: 24.7 us -> none  [the longest x1 17.6 us: shards(): lax.all_to_all(query_send, 'seq', split_axis=1, concat_axis=0, tiled=True)]
    all_gather x1 -> x0, waiting for transfers between devices: 16.1 us -> none  [shards(): lax.all_gather(key_grad, 'seq', axis=0, tiled=True)]
  transfers between devices with their start and end apart: 5 -> 0, of which waited for: 5 -> 0; matrix products, arithmetic and copies ran while one was open for 2% -> 0% of each run, Pallas kernels for 0% -> 0%
where the time goes in v1:
time: 93.3 us; the launch traced here: 93 us
  Pallas kernels  85 us (91%)
  local copies, waits for them, and re-layouts  7.38 us (8%)
    pallas_call x1, Pallas kernels, shards(): pl.pallas_call(functools.partial(kernel, (nx, ny, nz, rows, wide * width)...  85 us
    unnamed x14, local copies, waits for them, and re-layouts  7.38 us

profile of v1, /device:TPU:1, one launch (start us, length us, event | category | flops | bytes accessed | tf_op | source)
XLA Modules:
  0.0 93.0 jit_solution(16988806926708212798)
XLA Ops:
  0.6 0.0 copy-start.5
  0.6 0.6 copy-done.5
  1.3 0.0 copy-start
  1.3 1.2 %copy-done = bf16[1,128,4096]{2,1,0:T(8,128)(2,1)S(1)} copy-done((bf16[1,128,4096]{2,1,0:T(8,128)(2,1)S(1)}, bf16[1,128,4096]{2,1,0:T(8,128)(2,1)}, u32[]{:S(2)}) %copy-start) | copy-done | bytes 1048600
  2.5 0.0 copy-start.1
  2.5 1.2 %copy-done.1 = bf16[1,128,4096]{2,1,0:T(8,128)(2,1)S(1)} copy-done((bf16[1,128,4096]{2,1,0:T(8,128)(2,1)S(1)}, bf16[1,128,4096]{2,1,0:T(8,128)(2,1)}, u32[]{:S(2)}) %copy-start.1) | copy-done | bytes 1048600
  3.7 0.0 copy-start.2
  3.7 1.2 %copy-done.2 = bf16[1,128,4096]{2,1,0:T(8,128)(2,1)S(1)} copy-done((bf16[1,128,4096]{2,1,0:T(8,128)(2,1)S(1)}, bf16[1,128,4096]{2,1,0:T(8,128)(2,1)}, u32[]{:S(2)}) %copy-start.2) | copy-done | bytes 1048600
  5.0 0.0 copy-start.3
  5.0 0.9 copy-done.3
  5.9 0.0 copy-start.4
  5.9 0.9 copy-done.4
  6.8 85.0 %shard_map.77 = (bf16[128,512]{1,0:T(8,128)(2,1)S(1)}, f32[4,512]{1,0:T(4,128)S(1)}) custom-call(bf16[128,4096]{1,0:T(8,128)(2,1)S(1)} %bitcast.6, bf16[128,512]{1,0:T(8,128)(2,1)S(1)} %bitcast.9, bf16[128,512]{1,0:T(8,128)(2,1)S(1)} %bitcast.10, bf16[128,4096]{1,0:T(8,128)(2,1)S(1)} %bitcast.7, bf16[128,4096]{1,0:T(8,128)(2,1)S(1)} %bitcast.8, ...), custom_call_target="tpu_custom_call" | custom-call | tf_op jit(solution)/shard_map/pallas_call | solution.py:306
  91.8 0.7 copy.10
  92.4 0.6 copy.11
Async XLA Ops:
  0.6 0.7 copy-start.5
  1.3 1.2 %copy-start = (bf16[1,128,4096]{2,1,0:T(8,128)(2,1)S(1)}, bf16[1,128,4096]{2,1,0:T(8,128)(2,1)}, u32[]{:S(2)}) copy-start(bf16[1,128,4096]{2,1,0:T(8,128)(2,1)} %param.6) | copy-start | bytes 3145732
  2.5 1.2 %copy-start.1 = (bf16[1,128,4096]{2,1,0:T(8,128)(2,1)S(1)}, bf16[1,128,4096]{2,1,0:T(8,128)(2,1)}, u32[]{:S(2)}) copy-start(bf16[1,128,4096]{2,1,0:T(8,128)(2,1)} %param.9) | copy-start | bytes 3145732
  3.7 1.2 %copy-start.2 = (bf16[1,128,4096]{2,1,0:T(8,128)(2,1)S(1)}, bf16[1,128,4096]{2,1,0:T(8,128)(2,1)}, u32[]{:S(2)}) copy-start(bf16[1,128,4096]{2,1,0:T(8,128)(2,1)} %param.10) | copy-start | bytes 3145732
  5.0 0.9 copy-start.3
  5.9 0.9 copy-start.4

commit v2 on v1

v2 whole, which is shorter than its diff:
```python
import functools
import math

import jax
import jax.numpy as jnp
from jax import lax
from jax.experimental import pallas as pl
from jax.experimental.pallas import tpu as pltpu
from jax.sharding import PartitionSpec as P

HD = 128
KVH = 4
NEG_FILL = -1e30
MESH = pl.DeviceIdType.MESH
Z_CHIPS = 8
PARTS = 2

def kernel(
    dims, q_hbm, k_hbm, v_hbm, do_hbm, f_hbm, len_ref, kg_ref, w_ref,
    q_ref, k_ref, v_ref, do_ref, f_ref,
    k_prev, v_prev, grad_cols, key_own, back_send, back_recv,
    feat_cols, feat_send, pair_grad, weight, ring_send, ring_recv,
    mid_send, mid_recv, last_send, last_recv, sq_send, sq_recv,
    load_sems, halo_sems, feat_sems, back_sems, pair_sems, ring_sems, mid_sems, last_sems, sq_sems,
):
    nx, ny, nz, rows, entry_count = dims
    tok = q_ref.shape[0]
    width = k_ref.shape[1]
    heads = q_ref.shape[1] // width
    score_scale = 1.0 / math.sqrt(HD)
    f32, bf16 = jnp.float32, jnp.bfloat16

    seq, dp = lax.axis_index("seq"), lax.axis_index("dp")
    x, core = seq // 2, seq % 2
    y, z = dp // nz, dp % nz
    count = nx * 2
    left = (lax.rem(seq + count - 1, count), dp)
    partner = (x * 2 + 1 - core, dp)

    def at_seq(step):
        return (lax.rem(seq + step, count), dp)

    def at_x(step):
        return (lax.rem(x + step, nx) * 2 + core, dp)

    def at_y(step):
        return (seq, lax.rem(y + step, ny) * nz + z)

    def at_z(step):
        return (seq, y * nz + lax.rem(z + step, nz))

    barrier = pltpu.get_barrier_semaphore()
    for where_to, size in ((at_seq, count), (at_y, ny), (at_z, nz)):
        def greet(step, carry, where_to=where_to):
            pl.semaphore_signal(barrier, inc=1, device_id=where_to(step), device_id_type=MESH)
            return carry
        lax.fori_loop(1, size, greet, 0)

    pairs = ((k_hbm, k_ref), (v_hbm, v_ref), (f_hbm, f_ref), (q_hbm, q_ref), (do_hbm, do_ref))
    loads = [pltpu.make_async_copy(src, dst, load_sems.at[i]) for i, (src, dst) in enumerate(pairs)]
    for load in loads:
        load.start()

    def remote(src, dst, sems, place, target):
        return pltpu.make_async_remote_copy(
            src_ref=src, dst_ref=dst, send_sem=sems.at[(0,) + place], recv_sem=sems.at[(1,) + place],
            device_id=target, device_id_type=MESH,
        )

    def group_cols(group):
        return pl.ds(group * HD, HD)

    def halo_copies(group):
        cols = group_cols(group)
        return (
            remote(k_ref.at[:, cols], k_prev.at[:, cols], halo_sems, (0, group), at_seq(1)),
            remote(v_ref.at[:, cols], v_prev.at[:, cols], halo_sems, (1, group), at_seq(1)),
        )

    feat_copy = remote(feat_send, feat_cols.at[:, :, pl.ds(tok, tok)], feat_sems, (0,), partner)

    loads[0].wait()
    loads[1].wait()
    pl.semaphore_wait(barrier, (count - 1) + (ny - 1) + (nz - 1))
    for group in range(KVH):
        for copy in halo_copies(group):
            copy.start()

    query_pos = seq * tok + lax.broadcasted_iota(jnp.int32, (1, tok), 1)
    key_pos = (seq - 1) * tok + lax.broadcasted_iota(jnp.int32, (2 * tok, tok), 0)

    def doc_start(doc, carry):
        total, start = carry
        total = total + len_ref[0, doc]
        return total, jnp.where(query_pos >= total, total, start)

    first_key = lax.fori_loop(0, len_ref.shape[1], doc_start, (jnp.int32(0), jnp.zeros((1, tok), jnp.int32)))[1]
    visible = (key_pos >= first_key) & (key_pos <= query_pos)

    loads[2].wait()
    span = feat_cols.shape[1]

    def turn(block, carry):
        here = pl.multiple_of((block * 2 + core) * span, 128)
        there = pl.multiple_of((block * 2 + 1 - core) * span, 128)
        feat_send[block] = f_ref[:, pl.ds(there, span)].T
        feat_cols[block, :, 0:tok] = f_ref[:, pl.ds(here, span)].T
        return carry

    lax.fori_loop(0, nx, turn, 0)
    feat_copy.start()
    loads[3].wait()
    loads[4].wait()

    def back_copy(group):
        return remote(back_send.at[group], back_recv.at[group], back_sems, (group,), left)

    def attend(group):
        cols = group_cols(group)
        for copy in halo_copies(group):
            copy.wait_recv()
        keys = jnp.concatenate([k_prev[:, cols], k_ref[:, cols]], axis=0)
        values = jnp.concatenate([v_prev[:, cols], v_ref[:, cols]], axis=0)
        queries = []
        for head in range(heads):
            at = pl.ds((group * heads + head) * HD, HD)
            query = q_ref[:, at]
            queries.append(query)
            scores = lax.dot_general(
                keys, query, (((1,), (1,)), ((), ())), preferred_element_type=f32
            ) * score_scale
            grad_weights = lax.dot_general(
                values, do_ref[:, at], (((1,), (1,)), ((), ())), preferred_element_type=f32
            )
            scores = jnp.where(visible, scores, NEG_FILL)
            exponent = jnp.exp(scores - jnp.max(scores, axis=0, keepdims=True))
            attention = exponent * (1.0 / jnp.sum(exponent, axis=0, keepdims=True))
            row_delta = jnp.sum(attention * grad_weights, axis=0, keepdims=True)
            grad_cols[:, head * HD:(head + 1) * HD] = (
                attention * (grad_weights - row_delta) * score_scale
            ).astype(bf16)
        key_part = jnp.dot(
            grad_cols[...], jnp.concatenate(queries, axis=0), preferred_element_type=f32
        )
        back_send[group] = key_part[:tok].astype(bf16)
        back_copy(group).start()
        key_own[:, cols] = key_part[tok:]

    def pair_copy(group):
        cols = group_cols(group)
        return remote(
            pair_grad.at[pl.ds(0, tok), cols], pair_grad.at[pl.ds(tok, tok), cols],
            pair_sems, (group,), partner,
        )

    def add_back(group):
        cols = group_cols(group)
        back_copy(group).wait_recv()
        done = (key_own[:, cols] + back_recv[group].astype(f32)).astype(bf16)
        pair_grad[0:tok, cols] = done
        pair_copy(group).start()
        kg_ref[:, cols] = done

    def multiply(group):
        pair_copy(group).wait_recv()
        grads = pair_grad[:, group_cols(group)]

        def one_block(block, carry):
            weight[group, block] = jnp.dot(
                feat_cols[block], grads, preferred_element_type=f32
            ).reshape(weight.shape[2:])
            return carry

        lax.fori_loop(0, nx, one_block, 0)

    sides = (
        (nx, ny, at_x, at_y, x, y),
        (ny, nx, at_y, at_x, y, x),
    )

    def parts(group):
        other = sides[group % 2][1]
        cut = PARTS if other % PARTS == 0 else 1
        return [(part, pl.ds(part * (other // cut), other // cut)) for part in range(cut)]

    def own_term(group, away, some):
        size, mine = sides[group % 2][0], sides[group % 2][4]
        place = lax.rem(mine + away + size, size)
        return weight[group, place, some] if group % 2 == 0 else weight[group, some, place]

    def reach(group, way):
        size = sides[group % 2][0]
        return size // 2 if way == 0 else (size - 1) // 2

    def ring_copy(group, way, part, some, step):
        size, _, where_to = sides[group % 2][:3]
        place = (group, way, step, some)
        return remote(
            ring_send.at[place], ring_recv.at[place], ring_sems, (group, way, step, part),
            where_to(size - 1) if way == 0 else where_to(1),
        )

    def ring_step(group, step):
        for part, some in parts(group):
            for way in range(2):
                far = reach(group, way)
                if step >= far:
                    continue
                term = own_term(group, (step - far) if way == 0 else (far - step), some)
                if step > 0:
                    ring_copy(group, way, part, some, step - 1).wait_recv()
                    term = term + ring_recv[group, way, step - 1, some].astype(f32)
                ring_send[group, way, step, some] = term.astype(bf16)
                ring_copy(group, way, part, some, step).start()

    def mid_copy(group, step):
        _, other, _, where_to, _, mine = sides[group % 2]
        return remote(
            mid_send.at[group, lax.rem(mine + step, other)], mid_recv.at[group, step],
            mid_sems, (group, step), where_to(step),
        )

    def ring_end(group):
        for part, some in parts(group):
            term = own_term(group, 0, some)
            for way in range(2):
                far = reach(group, way)
                if far:
                    ring_copy(group, way, part, some, far - 1).wait_recv()
                    term = term + ring_recv[group, way, far - 1, some].astype(f32)
            mid_send[group, some] = term.astype(bf16)

        def send_mid(step, carry):
            mid_copy(group, step).start()
            return carry

        lax.fori_loop(1, sides[group % 2][1], send_mid, 0)

    for group in range(KVH):
        attend(group)
        if group >= 1:
            add_back(group - 1)
        if group == 1:
            feat_copy.wait_recv()
        if group >= 2:
            multiply(group - 2)
            ring_step(group - 2, 0)
    ring_step(0, 1)
    add_back(KVH - 1)
    multiply(KVH - 2)
    ring_step(KVH - 2, 0)
    multiply(KVH - 1)
    ring_step(KVH - 1, 0)

    due = (6.8, 9.4, 11.3, 12.4)
    turns = []
    for group in range(KVH):
        last = max(reach(group, 0), reach(group, 1))
        for step in range(2 if group == 0 else 1, last + 1):
            turns.append((due[group] + 2.7 * step, group, step, step == last))
        if last == 0 or (group == 0 and last == 1):
            turns.append((due[group] + 2.7 * last, group, last, True))
    for _, group, step, end in sorted(turns):
        if end:
            ring_end(group)
        else:
            ring_step(group, step)

    sums = []
    for group in range(KVH):
        def add_mid(step, carry, group=group):
            mid_copy(group, step).wait_recv()
            return carry + mid_recv[group, step].astype(f32)
        mine = mid_send[group, sides[group % 2][5]].astype(f32)
        sums.append(lax.fori_loop(1, sides[group % 2][1], add_mid, mine))
    block = jnp.concatenate(sums, axis=1)

    for index in range(nz):
        last_send[index] = block[index * rows:(index + 1) * rows]

    def last_copy(step):
        return remote(
            last_send.at[lax.rem(z + step, nz)], last_recv.at[step], last_sems, (step,), at_z(step)
        )

    def send_last(step, carry):
        last_copy(step).start()
        return carry

    def add_last(step, carry):
        last_copy(step).wait_recv()
        return carry + last_recv[step]

    lax.fori_loop(1, nz, send_last, 0)
    own_rows = lax.fori_loop(1, nz, add_last, last_send[z])

    squares = jnp.sum(own_rows * own_rows, axis=0, keepdims=True)
    squares = jnp.broadcast_to(
        jnp.sum(squares.reshape(1, width // HD, HD), axis=1), (8, HD)
    )
    axes = ((at_z, nz), (at_y, ny), (at_seq, count))

    def sq_copy(stage, step):
        return remote(
            sq_send.at[stage], sq_recv.at[stage, step], sq_sems, (stage, step), axes[stage][0](step)
        )

    for stage, (_, size) in enumerate(axes):
        sq_send[stage] = squares
        def send_sq(step, carry, stage=stage):
            sq_copy(stage, step).start()
            return carry
        def add_sq(step, carry, stage=stage):
            sq_copy(stage, step).wait_recv()
            return carry + sq_recv[stage, step]
        lax.fori_loop(1, size, send_sq, 0)
        squares = lax.fori_loop(1, size, add_sq, squares)
    total = jnp.sum(squares[0:1], axis=1, keepdims=True)
    root_mean = jnp.sqrt(total / entry_count + 1e-06)
    w_ref[...] = own_rows * jnp.minimum(1.0, 1.0 / root_mean)

    feat_copy.wait_send()
    for group in range(KVH):
        for copy in halo_copies(group):
            copy.wait_send()
        back_copy(group).wait_send()
        pair_copy(group).wait_send()
        for part, some in parts(group):
            for way in range(2):
                for step in range(reach(group, way)):
                    ring_copy(group, way, part, some, step).wait_send()
        def end_mid(step, carry, group=group):
            mid_copy(group, step).wait_send()
            return carry
        lax.fori_loop(1, sides[group % 2][1], end_mid, 0)

    def end_last(step, carry):
        last_copy(step).wait_send()
        return carry

    lax.fori_loop(1, nz, end_last, 0)
    for stage, (_, size) in enumerate(axes):
        def end_sq(step, carry, stage=stage):
            sq_copy(stage, step).wait_send()
            return carry
        lax.fori_loop(1, size, end_sq, 0)


def shards(sizes, queries, keys, values, grad_out, features, doc_lengths):
    seq_count, dp_count = sizes
    nz = min(Z_CHIPS, dp_count)
    nx, ny = seq_count // 2, dp_count // nz
    tok, wide = features.shape[1:]
    width = keys.shape[2]
    rows = wide // (seq_count * dp_count)
    low = nz * rows
    most = max(nx, ny)
    dma = pltpu.SemaphoreType.DMA
    vmem = pl.BlockSpec(memory_space=pltpu.VMEM)
    bf16, f32 = jnp.bfloat16, jnp.float32
    key_grad, clipped = pl.pallas_call(
        functools.partial(kernel, (nx, ny, nz, rows, wide * width)),
        out_shape=(
            jax.ShapeDtypeStruct((tok, width), bf16),
            jax.ShapeDtypeStruct((rows, width), f32),
        ),
        in_specs=[pl.BlockSpec(memory_space=pltpu.HBM)] * 5 + [pl.BlockSpec(memory_space=pltpu.SMEM)],
        out_specs=(vmem, vmem),
        scratch_shapes=[
            pltpu.VMEM((tok, queries.shape[2]), bf16),
            pltpu.VMEM((tok, width), bf16),
            pltpu.VMEM((tok, width), bf16),
            pltpu.VMEM((tok, queries.shape[2]), bf16),
            pltpu.VMEM((tok, wide), bf16),
            pltpu.VMEM((tok, width), bf16),
            pltpu.VMEM((tok, width), bf16),
            pltpu.VMEM((2 * tok, queries.shape[2] // KVH), bf16),
            pltpu.VMEM((tok, width), f32),
            pltpu.VMEM((KVH, tok, HD), bf16),
            pltpu.VMEM((KVH, tok, HD), bf16),
            pltpu.VMEM((nx, ny * low, 2 * tok), bf16),
            pltpu.VMEM((nx, ny * low, tok), bf16),
            pltpu.VMEM((2 * tok, width), bf16),
            pltpu.VMEM((KVH, nx, ny, low, HD), f32),
            pltpu.VMEM((KVH, 2, most // 2, most, low, HD), bf16),
            pltpu.VMEM((KVH, 2, most // 2, most, low, HD), bf16),
            pltpu.VMEM((KVH, most, low, HD), bf16),
            pltpu.VMEM((KVH, most, low, HD), bf16),
            pltpu.VMEM((nz, rows, width), f32),
            pltpu.VMEM((nz, rows, width), f32),
            pltpu.VMEM((3, 8, HD), f32),
            pltpu.VMEM((3, max(seq_count, ny, nz), 8, HD), f32),
            dma((5,)),
            dma((2, 2, KVH)),
            dma((2, 1)),
            dma((2, KVH)),
            dma((2, KVH)),
            dma((2, KVH, 2, most // 2, PARTS)),
            dma((2, KVH, most)),
            dma((2, nz)),
            dma((2, 3, max(seq_count, ny, nz))),
        ],
        compiler_params=pltpu.CompilerParams(
            collective_id=0, has_side_effects=True, vmem_limit_bytes=60 << 20
        ),
    )(queries[0], keys[0], values[0], grad_out[0], features[0], doc_lengths)
    return key_grad[None], clipped


def solution(mesh):
    in_specs = (
        P("dp", "seq", None),
        P("dp", "seq", None),
        P("dp", "seq", None),
        P("dp", "seq", None),
        P("dp", "seq", None),
        P("dp", None),
    )
    out_specs = (P("dp", "seq", None), P(("seq", "dp"), None))
    return jax.shard_map(
        functools.partial(shards, (mesh.shape["seq"], mesh.shape["dp"])),
        mesh=mesh, in_specs=in_specs, out_specs=out_specs, check_vma=False,
    )
```

time: 93.3 us -> 87.2 us (0.935)
  local copies, waits for them, and re-layouts: 7.38 us -> 2.18 us
    unnamed x14 -> x4, local copies, waits for them, and re-layouts: 7.38 us -> 2.18 us
where the time goes in v2:
time: 87.2 us; the launch traced here: 87 us
  Pallas kernels  84.2 us (97%)
  local copies, waits for them, and re-layouts  2.18 us (3%)
    pallas_call x1, Pallas kernels, shards(): pl.pallas_call(functools.partial(kernel, (nx, ny, nz, rows, wide * width)...  84.2 us
    unnamed x4, local copies, waits for them, and re-layouts  2.18 us

profile of v2, /device:TPU:1, one launch (start us, length us, event | category | flops | bytes accessed | tf_op | source)
XLA Modules:
  0.0 87.0 jit_solution(13938531205369792546)
XLA Ops:
  0.6 84.2 %shard_map.77 = (bf16[128,512]{1,0:T(8,128)(2,1)}, f32[4,512]{1,0:T(4,128)}) custom-call(bf16[128,4096]{1,0:T(8,128)(2,1)} %bitcast.6, bf16[128,512]{1,0:T(8,128)(2,1)} %bitcast.9, bf16[128,512]{1,0:T(8,128)(2,1)} %bitcast.10, bf16[128,4096]{1,0:T(8,128)(2,1)} %bitcast.7, bf16[128,4096]{1,0:T(8,128)(2,1)} %bitcast.8, s32[1,32]{1,0:T(1,128)} %len_ref.1), custom_call_target="tpu_custom_call" | custom-call | tf_op jit(solution)/shard_map/pallas_call | solution.py:361
  84.8 0.0 copy-start
  84.8 1.6 %copy.10 = bf16[1,128,512]{2,1,0:T(8,128)(2,1)} copy(bf16[1,128,512]{2,1,0:T(8,128)(2,1)} %bitcast.11) | data formatting | bytes 262144
  86.4 0.0 copy-done
  86.4 0.6 copy.11
Async XLA Ops:
  84.8 1.6 %copy-start = (f32[4,512]{1,0:T(4,128)S(1)}, f32[4,512]{1,0:T(4,128)}, u32[]{:S(2)}) copy-start(f32[4,512]{1,0:T(4,128)} %get-tuple-element.9) | copy-start | bytes 24580
